TPU v7x, 128 devices: a whole 4x4x4 slice. The times are simulated.
128 devices in a mesh: ctx: 8 (over x, y_lo), ffn: 16 (over z, y_hi, core).
Axes of the slice: x: 4, y: 4 (y_hi: 2, y_lo: 2; y = y_hi * 2 + y_lo), z: 4, core: 2. Of those that a mesh axis runs over, the one named last changes fastest.
Arguments:
- resid_in: bfloat16 [1024, 4096], P(('ctx', 'ffn')), may hold values from -6 to 6
- queries: bfloat16 [1024, 4096], P('ctx', 'ffn'), may hold values from -6 to 6
- keys_in: bfloat16 [1024, 1024], P('ctx'), may hold values from -6 to 6
- value_rows_input: bfloat16 [1024, 1024], P('ctx'), may hold values from -6 to 6
- w_out: bfloat16 [4096, 4096], P('ffn'), may hold values from -0.09375 to 0.09375
- norm_gain: float32 [4096], replicated, may hold values from 0.5 to 1.5
- w_gate: bfloat16 [4096, 7168], P(None, 'ffn'), may hold values from -0.09375 to 0.09375
- w_up: bfloat16 [4096, 7168], P(None, 'ffn'), may hold values from -0.09375 to 0.09375
- w_down: bfloat16 [7168, 4096], P('ffn'), may hold values from -0.0625 to 0.0625
- cotangent: bfloat16 [1024, 4096], P(('ctx', 'ffn')), may hold values from -6 to 6
- positions: int32 [1024], P('ctx'), may hold values from 0 to 1023, as said below
- doc_ids: int32 [1024], replicated, may hold values from 0 to 3, never falling along the last dimension, each value on 1 to 512 neighbouring positions
Outputs:
- mixed: bfloat16 [1024, 4096], P(('ctx', 'ffn'))
- grad_resid: bfloat16 [1024, 4096], P(('ctx', 'ffn'))
- grad_queries: bfloat16 [1024, 4096], P('ctx', 'ffn')
- key_gradient_rows: float32 [1024, 1024], P(('ctx', 'ffn'))
- value_gradient_rows: float32 [1024, 1024], P(('ctx', 'ffn'))
- grad_gain: float32 [4096], replicated
- grad_w_out: float32 [4096, 4096], P('ffn', 'ctx')
- grad_w_gate: float32 [4096, 7168], P('ctx', 'ffn')
- grad_w_up: float32 [4096, 7168], P('ctx', 'ffn')
- grad_w_down: float32 [7168, 4096], P('ffn', 'ctx')
Inputs may be any that keep to these rules, and one draw needn't show every extreme that they name: Each aligned block of 64 rows holds 64 consecutive positions in rising order, and every position occurs once.
All inputs are finite; a program needn't handle non-finite values.
Results may differ from a plain program's by a relative error of at most 0.033.
Values may be sent and summed in bfloat16 or wider, within the bound.
A program may use at most 128 MiB of HBM per device.

v0:
```python
import math
import jax
import jax.numpy as jnp
from jax import lax
from jax.sharding import PartitionSpec as P

QUERY_HEADS = 32
KEY_VALUE_HEADS = 8
HEAD_WIDTH = 128
masked_fill = -1e30
norm_eps = 1e-05


def passed_along(value, axis, by):
    count = lax.axis_size(axis)
    return lax.ppermute(value, axis, [(i, (i + by) % count) for i in range(count)])


def tile_visible(query_pos, query_seg, key_pos, key_seg):
    return (key_pos[None, :] <= query_pos[:, None]) & (key_seg[None, :] == query_seg[:, None])


def forward_tile(folded, q_heads, key_piece, value_piece, visible, score_scale):
    row_max, row_total, accumulated = folded
    scores = (
        jnp.einsum("rhd,kd->hrk", q_heads, key_piece, preferred_element_type=jnp.float32)
        * score_scale
    )
    scores = jnp.where(visible[None], scores, masked_fill)
    new_max = jnp.maximum(row_max, jnp.max(scores, axis=2))
    weights = jnp.where(visible[None], jnp.exp(scores - new_max[:, :, None]), 0.0)
    shrink = jnp.exp(row_max - new_max)
    new_total = row_total * shrink + jnp.sum(weights, axis=2)
    product = jnp.einsum(
        "hrk,kd->hrd", weights.astype(jnp.bfloat16), value_piece, preferred_element_type=jnp.float32
    )
    return (new_max, new_total, accumulated * shrink[:, :, None] + product)


def row_contract(left_rows, right_rows):
    return jnp.einsum("rd,rf->df", left_rows, right_rows, preferred_element_type=jnp.float32)


def body(
    resid_in,
    queries,
    keys_in,
    value_rows_input,
    w_out,
    norm_gain,
    w_gate,
    w_up,
    w_down,
    cotangent,
    positions,
    doc_ids,
):
    row_count = queries.shape[0]
    resident_heads = queries.shape[1] // HEAD_WIDTH
    ctx_size = lax.axis_size("ctx")
    ctx_index = lax.axis_index("ctx")
    key_value_group = lax.axis_index("ffn") * resident_heads // (QUERY_HEADS // KEY_VALUE_HEADS)
    score_scale = 1.0 / math.sqrt(HEAD_WIDTH)
    all_pos = lax.all_gather(positions, "ctx", axis=0, tiled=True)
    all_seg = doc_ids[all_pos]
    own_seg = doc_ids[positions]
    key_own = lax.dynamic_slice_in_dim(keys_in, key_value_group * HEAD_WIDTH, HEAD_WIDTH, 1)
    value_own = lax.dynamic_slice_in_dim(
        value_rows_input, key_value_group * HEAD_WIDTH, HEAD_WIDTH, 1
    )
    kv_pair = jnp.stack((key_own, value_own), axis=1)
    q_heads = queries.reshape(row_count, resident_heads, HEAD_WIDTH)

    def key_visible(row_start, row_num):
        return tile_visible(
            positions,
            own_seg,
            lax.dynamic_slice_in_dim(all_pos, row_start, row_num, 0),
            lax.dynamic_slice_in_dim(all_seg, row_start, row_num, 0),
        )

    def fold_keys(folded, shard_rows, row_start):
        visible = key_visible(row_start, shard_rows.shape[0])
        return forward_tile(
            folded, q_heads, shard_rows[:, 0], shard_rows[:, 1], visible, score_scale
        )

    start_state = (
        jnp.full((resident_heads, row_count), masked_fill, jnp.float32),
        jnp.zeros((resident_heads, row_count), jnp.float32),
        jnp.zeros((resident_heads, row_count, HEAD_WIDTH), jnp.float32),
    )

    def pass_step(turn_index, running):
        folded, travel = running
        travel = passed_along(travel, "ctx", 1)
        source = (ctx_index - turn_index - 1) % ctx_size
        return (fold_keys(folded, travel, source * row_count), travel)

    first_state = fold_keys(start_state, kv_pair, ctx_index * row_count)
    (row_max, row_total, accumulated), unused = lax.fori_loop(
        0, ctx_size - 1, pass_step, (first_state, kv_pair)
    )
    attended = (accumulated / row_total[:, :, None]).astype(jnp.bfloat16)
    log_totals = row_max + jnp.log(row_total)
    attended_rows = jnp.transpose(attended, (1, 0, 2)).reshape(
        row_count, resident_heads * HEAD_WIDTH
    )
    projected = lax.psum_scatter(
        jnp.dot(attended_rows, w_out, preferred_element_type=jnp.float32).astype(jnp.bfloat16),
        "ffn",
        scatter_dimension=0,
        tiled=True,
    ).astype(jnp.float32)
    hidden_bf = (resid_in.astype(jnp.float32) + projected).astype(jnp.bfloat16)
    hidden_f = lax.optimization_barrier(hidden_bf).astype(jnp.float32)
    inv_rms = lax.rsqrt(jnp.mean(hidden_f * hidden_f, axis=1, keepdims=True) + norm_eps)
    normed = (hidden_f * inv_rms * norm_gain).astype(jnp.bfloat16)
    normed_rows = lax.all_gather(normed, "ffn", axis=0, tiled=True)
    gate_pre = jnp.dot(normed_rows, w_gate, preferred_element_type=jnp.float32)
    up_proj = jnp.dot(normed_rows, w_up, preferred_element_type=jnp.float32)
    gate_sig = jax.nn.sigmoid(gate_pre)
    activated = (gate_pre * gate_sig * up_proj).astype(jnp.bfloat16)
    mixed = (
        hidden_f
        + lax.psum_scatter(
            jnp.dot(activated, w_down, preferred_element_type=jnp.float32).astype(jnp.bfloat16),
            "ffn",
            scatter_dimension=0,
            tiled=True,
        ).astype(jnp.float32)
    ).astype(jnp.bfloat16)
    cot_rows = lax.all_gather(cotangent, "ffn", axis=0, tiled=True)
    grad_act = jnp.dot(cot_rows, w_down.T, preferred_element_type=jnp.float32)
    grad_up = (grad_act * gate_pre * gate_sig).astype(jnp.bfloat16)
    grad_gate = (grad_act * up_proj * gate_sig * (1.0 + gate_pre * (1.0 - gate_sig))).astype(
        jnp.bfloat16
    )
    grad_normed = lax.psum_scatter(
        (
            jnp.dot(grad_gate, w_gate.T, preferred_element_type=jnp.float32)
            + jnp.dot(grad_up, w_up.T, preferred_element_type=jnp.float32)
        ).astype(jnp.bfloat16),
        "ffn",
        scatter_dimension=0,
        tiled=True,
    ).astype(jnp.float32)
    gained = grad_normed * norm_gain
    inv_cube = inv_rms * inv_rms * inv_rms
    grad_resid = (
        cotangent.astype(jnp.float32)
        + inv_rms * gained
        - hidden_f * inv_cube * jnp.mean(gained * hidden_f, axis=1, keepdims=True)
    ).astype(jnp.bfloat16)
    grad_gain = lax.psum(jnp.sum(grad_normed * hidden_f * inv_rms, axis=0), ("ctx", "ffn"))
    grad_rows = lax.all_gather(grad_resid, "ffn", axis=0, tiled=True)
    grad_attended = jnp.dot(grad_rows, w_out.T, preferred_element_type=jnp.float32).astype(
        jnp.bfloat16
    )
    grad_heads = grad_attended.reshape(row_count, resident_heads, HEAD_WIDTH)
    deltas = jnp.sum(
        grad_heads.astype(jnp.float32)
        * attended_rows.reshape(row_count, resident_heads, HEAD_WIDTH).astype(jnp.float32),
        axis=2,
    )
    delta_heads = deltas.T
    stats_all, deltas_all = (
        lax.all_gather(log_totals.T, "ctx", axis=0, tiled=True),
        lax.all_gather(deltas, "ctx", axis=0, tiled=True),
    )
    shard_rows = lax.all_gather(kv_pair, "ctx", axis=0, tiled=True)
    key_piece = shard_rows[:, 0]
    value_piece = shard_rows[:, 1]
    visible = key_visible(jnp.int32(0), shard_rows.shape[0])

    def update(running):
        scores = (
            jnp.einsum("rhd,kd->hrk", q_heads, key_piece, preferred_element_type=jnp.float32)
            * score_scale
        )
        scores = jnp.where(visible[None], scores, masked_fill)
        prob_weights = jnp.where(visible[None], jnp.exp(scores - log_totals[:, :, None]), 0.0)
        grad_probs = jnp.einsum(
            "rhd,kd->hrk", grad_heads, value_piece, preferred_element_type=jnp.float32
        )
        grad_scores = (prob_weights * (grad_probs - delta_heads[:, :, None])).astype(jnp.bfloat16)
        return (
            jnp.einsum("hrk,kd->rhd", grad_scores, key_piece, preferred_element_type=jnp.float32)
            * score_scale
        )

    grad_query = update(jnp.zeros((row_count, resident_heads, HEAD_WIDTH), jnp.float32))
    zero_block = jnp.zeros((row_count, HEAD_WIDTH), jnp.float32)
    shard_rows = (
        lax.all_gather(queries, "ctx", axis=0, tiled=True),
        lax.all_gather(grad_attended, "ctx", axis=0, tiled=True),
    )
    row_num = shard_rows[0].shape[0]
    q_piece = shard_rows[0].reshape(row_num, resident_heads, HEAD_WIDTH)
    g_piece = shard_rows[1].reshape(row_num, resident_heads, HEAD_WIDTH)
    fold_visible = tile_visible(all_pos, all_seg, positions, own_seg)
    stat_piece = stats_all.T
    delta_piece = deltas_all.T

    def update(running):
        scores = (
            jnp.einsum("qhd,kd->hqk", q_piece, key_own, preferred_element_type=jnp.float32)
            * score_scale
        )
        scores = jnp.where(fold_visible[None], scores, masked_fill)
        prob_weights = jnp.where(fold_visible[None], jnp.exp(scores - stat_piece[:, :, None]), 0.0)
        grad_probs = jnp.einsum(
            "qhd,kd->hqk", g_piece, value_own, preferred_element_type=jnp.float32
        )
        grad_scores = (prob_weights * (grad_probs - delta_piece[:, :, None])).astype(jnp.bfloat16)
        grad_key = (
            jnp.einsum("hqk,qhd->kd", grad_scores, q_piece, preferred_element_type=jnp.float32)
            * score_scale
        )
        grad_value = jnp.einsum(
            "hqk,qhd->kd",
            prob_weights.astype(jnp.bfloat16),
            g_piece,
            preferred_element_type=jnp.float32,
        )
        return (grad_key, grad_value)

    grad_key_own, grad_value_own = update((zero_block, zero_block))
    empty_rows = jnp.zeros((row_count, keys_in.shape[1]), jnp.float32)
    placed_key = lax.dynamic_update_slice_in_dim(
        empty_rows, grad_key_own, key_value_group * HEAD_WIDTH, 1
    )
    placed_value = lax.dynamic_update_slice_in_dim(
        empty_rows, grad_value_own, key_value_group * HEAD_WIDTH, 1
    )
    key_gradient_rows, value_gradient_rows = (
        lax.psum_scatter(
            placed_key.astype(jnp.bfloat16), "ffn", scatter_dimension=0, tiled=True
        ).astype(jnp.float32),
        lax.psum_scatter(
            placed_value.astype(jnp.bfloat16), "ffn", scatter_dimension=0, tiled=True
        ).astype(jnp.float32),
    )
    row_terms = (row_contract(normed_rows, grad_gate), row_contract(normed_rows, grad_up))
    grad_w_gate, grad_w_up = (
        lax.psum_scatter(
            row_terms[0].astype(jnp.bfloat16), "ctx", scatter_dimension=0, tiled=True
        ).astype(jnp.float32),
        lax.psum_scatter(
            row_terms[1].astype(jnp.bfloat16), "ctx", scatter_dimension=0, tiled=True
        ).astype(jnp.float32),
    )
    col_terms = (row_contract(attended_rows, grad_rows), row_contract(activated, cot_rows))
    grad_w_out, grad_w_down = (
        lax.psum_scatter(
            col_terms[0].astype(jnp.bfloat16), "ctx", scatter_dimension=1, tiled=True
        ).astype(jnp.float32),
        lax.psum_scatter(
            col_terms[1].astype(jnp.bfloat16), "ctx", scatter_dimension=1, tiled=True
        ).astype(jnp.float32),
    )
    grad_queries = grad_query.reshape(row_count, resident_heads * HEAD_WIDTH).astype(jnp.bfloat16)
    return (
        mixed,
        grad_resid,
        grad_queries,
        key_gradient_rows,
        value_gradient_rows,
        grad_gain,
        grad_w_out,
        grad_w_gate,
        grad_w_up,
        grad_w_down,
    )


def solution(mesh):
    return jax.shard_map(
        body,
        mesh=mesh,
        in_specs=(
            P(("ctx", "ffn"), None),
            P("ctx", "ffn"),
            P("ctx", None),
            P("ctx", None),
            P("ffn", None),
            P(),
            P(None, "ffn"),
            P(None, "ffn"),
            P("ffn", None),
            P(("ctx", "ffn"), None),
            P("ctx"),
            P(),
        ),
        out_specs=(
            P(("ctx", "ffn"), None),
            P(("ctx", "ffn"), None),
            P("ctx", "ffn"),
            P(("ctx", "ffn"), None),
            P(("ctx", "ffn"), None),
            P(),
            P("ffn", "ctx"),
            P("ctx", "ffn"),
            P("ctx", "ffn"),
            P("ffn", "ctx"),
        ),
        check_vma=False,
    )
```

profile of v0, /device:TPU:32, one launch (start us, length us, event | category | flops | bytes accessed | tf_op | source)
XLA Modules:
  0.0 941.2 jit_solution(1435505484392055501)
XLA Ops:
  9.0 19.0 %all-gather = s32[8,1,128]{2,1,0:T(1,128)S(1)} all-gather(s32[1,1,128]{2,1,0:T(1,128)} %bitcast.186), channel_id=1, replica_groups=mesh['ctx'=8,'ffn'=16] {'ctx'}, dimensions={0}, use_global_device_ids=true | all-gather | bytes 4608 | tf_op jit(solution)/shard_map/all_gather | solution.py:64
  39.2 49.3 %while.21 = (s32[]{:T(128)}, f32[2,128]{1,0:T(2,128)S(1)}, f32[2,128]{1,0:T(2,128)S(1)}, f32[2,128,128]{2,1,0:T(8,128)S(1)}, bf16[128,2,128]{2,0,1:T(8,128)(2,1)...) while((s32[]{:T(128)}, f32[2,128]{1,0:T(2,128)S(1)}, ...), condition=%wide.region_5.6_spmd, body=%wide.region_2.5_spmd.sunk | while | flops 17187348 | bytes 1266056 | solution.py:101
  39.5 6.1 collective-permute-done
  46.5 6.6 collective-permute-done
  54.0 6.1 collective-permute-done
  61.0 6.1 collective-permute-done
  74.9 6.1 collective-permute-done
  81.9 6.1 collective-permute-done
  90.2 66.2 %reduce-scatter.10.cloned.1.call-done = bf16[8,4096]{1,0:T(8,128)(2,1)} async-done(((bf16[128,4096]{1,0:T(8,128)(2,1)}), bf16[8,4096]{1,0:T(8,128)(2,1)}) %reduce-scatter.10.cloned.1.call-update) | async-done | bytes 65552 | tf_op jit(solution)/shard_map/reduce_scatter | solution.py:109
  159.5 43.9 %all-gather.5.cloned.1.call-done = bf16[128,4096]{1,0:T(8,128)(2,1)} async-done(((bf16[8,4096]{1,0:T(8,128)(2,1)}), bf16[128,4096]{1,0:T(8,128)(2,1)}) %all-gather.5.cloned.1.call-update) | async-done | bytes 1048592 | tf_op jit(solution)/shard_map/all_gather | solution.py:119
  209.5 40.0 %all-gather.7.cloned.1.call-done = bf16[128,4096]{1,0:T(8,128)(2,1)} async-done(((bf16[8,4096]{1,0:T(8,128)(2,1)}), bf16[128,4096]{1,0:T(8,128)(2,1)}) %all-gather.7.cloned.1.call-update) | async-done | bytes 1048592 | tf_op jit(solution)/shard_map/all_gather | solution.py:133
  261.7 62.2 %reduce-scatter.14.cloned.1.call-done = bf16[8,4096]{1,0:T(8,128)(2,1)} async-done(((bf16[128,4096]{1,0:T(8,128)(2,1)}), bf16[8,4096]{1,0:T(8,128)(2,1)}) %reduce-scatter.14.cloned.1.call-update) | async-done | bytes 65552 | tf_op jit(solution)/shard_map/reduce_scatter | solution.py:139
  325.9 67.8 %reduce-scatter.12.cloned.1.call-done = bf16[8,4096]{1,0:T(8,128)(2,1)} async-done(((bf16[128,4096]{1,0:T(8,128)(2,1)}), bf16[8,4096]{1,0:T(8,128)(2,1)}) %reduce-scatter.12.cloned.1.call-update) | async-done | bytes 65552 | tf_op jit(solution)/shard_map/reduce_scatter | solution.py:126
  395.5 17.8 %all_gather.33 = f32[1024,2]{0,1:T(2,128)S(1)} all-gather(f32[128,2]{0,1:T(2,128)S(1)} %bitcast.190), channel_id=1, replica_groups=mesh['ctx'=8,'ffn'=16] {'ctx'}, dimensions={0}, use_global_device_ids=true | all-gather | bytes 9216 | tf_op jit(solution)/shard_map/all_gather | solution.py:168
  414.2 24.7 %all_gather.32 = bf16[1024,256]{0,1:T(8,128)(2,1)S(1)} all-gather(bf16[128,256]{0,1:T(8,128)(2,1)S(1)} %copy.44), channel_id=1, replica_groups=mesh['ctx'=8,'ffn'=16] {'ctx'}, dimensions={0}, use_global_device_ids=true | all-gather | bytes 589824 | tf_op jit(solution)/shard_map/all_gather | solution.py:195
  444.1 31.3 %all_gather.34 = bf16[1024,256]{1,0:T(8,128)(2,1)} all-gather(bf16[128,256]{1,0:T(8,128)(2,1)S(1)} %convolution_convert_fusion.6), channel_id=1, replica_groups=mesh['ctx'=8,'ffn'=16] {'ctx'}, dimensions={0}, use_global_device_ids=true | all-gather | bytes 589824 | tf_op jit(solution)/shard_map/all_gather | solution.py:196
  475.4 17.7 %all_gather.35 = f32[1024,2]{0,1:T(2,128)S(1)} all-gather(f32[128,2]{0,1:T(2,128)S(1)} %multiply_reduce_fusion), channel_id=1, replica_groups=mesh['ctx'=8,'ffn'=16] {'ctx'}, dimensions={0}, use_global_device_ids=true | all-gather | bytes 9216 | tf_op jit(solution)/shard_map/all_gather | solution.py:169
  515.1 29.1 %all_gather.30 = bf16[1024,2,128]{2,0,1:T(8,128)(2,1)S(1)} all-gather(bf16[128,2,128]{2,0,1:T(8,128)(2,1)S(1)} %copy-done.17), channel_id=1, replica_groups=mesh['ctx'=8,'ffn'=16] {'ctx'}, dimensions={0}, use_global_device_ids=true | all-gather | bytes 589824 | tf_op jit(solution)/shard_map/all_gather | solution.py:171
  546.2 62.7 %psum.7 = f32[4096]{0:T(1024)} all-reduce(f32[4096]{0:T(1024)S(1)} %copy-done.21), channel_id=1, replica_groups=mesh['ctx'=8,'ffn'=16] {'ctx','ffn'}, use_global_device_ids=true, to_apply=%region_15.16 | all-reduce | flops 4096 | bytes 32768 | tf_op jit(solution)/shard_map/psum | solution.py:155
  612.8 14.5 %reduce-scatter.18.cloned.1.call-done = bf16[8,1024]{1,0:T(8,128)(2,1)} async-done(((bf16[128,1024]{1,0:T(8,128)(2,1)}), bf16[8,1024]{1,0:T(8,128)(2,1)}) %reduce-scatter.18.cloned.1.call-update) | async-done | bytes 16400 | tf_op jit(solution)/shard_map/reduce_scatter | solution.py:240
  628.6 81.0 %reduce-scatter.22.cloned.1.call-done = bf16[512,448]{0,1:T(8,128)(2,1)} async-done(((bf16[4096,448]{0,1:T(8,128)(2,1)}), bf16[512,448]{0,1:T(8,128)(2,1)}) %reduce-scatter.22.cloned.1.call-update) | async-done | bytes 458768 | tf_op jit(solution)/shard_map/reduce_scatter | solution.py:246
  711.7 81.6 %reduce-scatter.24.cloned.1.call-done = bf16[512,448]{0,1:T(8,128)(2,1)} async-done(((bf16[4096,448]{0,1:T(8,128)(2,1)}), bf16[512,448]{0,1:T(8,128)(2,1)}) %reduce-scatter.24.cloned.1.call-update) | async-done | bytes 458768 | tf_op jit(solution)/shard_map/reduce_scatter | solution.py:249
  795.3 81.8 %reduce-scatter.26.cloned.1.call-done = bf16[448,512]{1,0:T(8,128)(2,1)} async-done(((bf16[448,4096]{1,0:T(8,128)(2,1)}), bf16[448,512]{1,0:T(8,128)(2,1)}) %reduce-scatter.26.cloned.1.call-update) | async-done | bytes 458768 | tf_op jit(solution)/shard_map/reduce_scatter | solution.py:258
  879.1 53.4 %reduce-scatter.20.cloned.1.call-done = bf16[256,512]{1,0:T(8,128)(2,1)} async-done(((bf16[256,4096]{1,0:T(8,128)(2,1)}), bf16[256,512]{1,0:T(8,128)(2,1)}) %reduce-scatter.20.cloned.1.call-update) | async-done | bytes 262160 | tf_op jit(solution)/shard_map/reduce_scatter | solution.py:255
  (220 shorter events, 94.4 us)
Async XLA Ops:
  7.2 81.5 %copy-start = (bf16[256,4096]{1,0:T(8,128)(2,1)S(1)}, bf16[256,4096]{1,0:T(8,128)(2,1)}, u32[]{:S(2)}) copy-start(bf16[256,4096]{1,0:T(8,128)(2,1)} %param.18) | copy-start | bytes 6291460
  7.2 149.3 %reduce-scatter.10.cloned.1.call-start = ((), (), s32[]{:S(2)}) async-start(), calls=%async_computation.9 | async-start | bytes 1114112 | tf_op jit(solution)/shard_map/reduce_scatter | solution.py:109
  39.2 6.4 collective-permute-start
  46.1 6.9 collective-permute-start
  53.6 6.4 collective-permute-start
  60.6 6.4 collective-permute-start
  67.6 6.4 collective-permute-start
  74.5 6.4 collective-permute-start
  81.5 6.4 collective-permute-start
  88.5 71.0 %copy-start.24 = (s32[128]{0:T(128)}, s32[128]{0:T(128)S(1)}, u32[]{:S(2)}) copy-start(s32[128]{0:T(128)S(1)} %get-tuple-element.564) | copy-start | bytes 1540
  88.5 324.8 %copy-start.22 = (s32[1024]{0:T(1024)}, s32[1024]{0:T(1024)S(1)}, u32[]{:S(2)}) copy-start(s32[1024]{0:T(1024)S(1)} %get-tuple-element.561) | copy-start | bytes 12292
  90.2 113.2 %all-gather.5.cloned.1.call-start = ((), (), s32[]{:S(2)}) async-start(), calls=%async_computation.10 | async-start | bytes 1114112 | tf_op jit(solution)/shard_map/all_gather | solution.py:119
  158.7 90.8 %all-gather.7.cloned.1.call-start = ((), (), s32[]{:S(2)}) async-start(), calls=%async_computation.12 | async-start | bytes 1114112 | tf_op jit(solution)/shard_map/all_gather | solution.py:133
  159.5 164.4 %reduce-scatter.14.cloned.1.call-start = ((), (), s32[]{:S(2)}) async-start(), calls=%async_computation.13 | async-start | bytes 1114112 | tf_op jit(solution)/shard_map/reduce_scatter | solution.py:139
  257.7 136.0 %copy-start.18 = (bf16[8,4096]{1,0:T(8,128)(2,1)S(1)}, bf16[8,4096]{1,0:T(8,128)(2,1)}, u32[]{:S(2)}) copy-start(bf16[8,4096]{1,0:T(8,128)(2,1)} %param.23) | copy-start | bytes 196612
  257.8 135.9 %reduce-scatter.12.cloned.1.call-start = ((), (), s32[]{:S(2)}) async-start(), calls=%async_computation.11 | async-start | bytes 1114112 | tf_op jit(solution)/shard_map/reduce_scatter | solution.py:126
  261.7 180.3 %all-gather.9.cloned.1.call-start = ((), (), s32[]{:S(2)}) async-start(), calls=%async_computation.14 | async-start | bytes 1114112 | tf_op jit(solution)/shard_map/all_gather | solution.py:156
  395.4 216.1 %reduce-scatter.16.cloned.1.call-start = ((), (), s32[]{:S(2)}) async-start(), calls=%async_computation.15 | async-start | bytes 278528 | tf_op jit(solution)/shard_map/reduce_scatter | solution.py:237
  496.0 131.2 %reduce-scatter.18.cloned.1.call-start = ((), (), s32[]{:S(2)}) async-start(), calls=%async_computation.16 | async-start | bytes 278528 | tf_op jit(solution)/shard_map/reduce_scatter | solution.py:240
  498.5 211.1 %reduce-scatter.22.cloned.1.call-start = ((), (), s32[]{:S(2)}) async-start(), calls=%async_computation.18 | async-start | bytes 4128768 | tf_op jit(solution)/shard_map/reduce_scatter | solution.py:246
  502.6 290.7 %reduce-scatter.24.cloned.1.call-start = ((), (), s32[]{:S(2)}) async-start(), calls=%async_computation.19 | async-start | bytes 4128768 | tf_op jit(solution)/shard_map/reduce_scatter | solution.py:249
  506.4 370.6 %reduce-scatter.26.cloned.1.call-start = ((), (), s32[]{:S(2)}) async-start(), calls=%async_computation.20 | async-start | bytes 4128768 | tf_op jit(solution)/shard_map/reduce_scatter | solution.py:258
  510.7 98.2 %copy-start.15 = (bf16[128,256]{0,1:T(8,128)(2,1)S(1)}, bf16[128,256]{0,1:T(8,128)(2,1)}, u32[]{:S(2)}) copy-start(bf16[128,256]{0,1:T(8,128)(2,1)} %copy-done.14) | copy-start | bytes 196612
  510.7 421.8 %reduce-scatter.20.cloned.1.call-start = ((), (), s32[]{:S(2)}) async-start(), calls=%async_computation.17 | async-start | bytes 2359296 | tf_op jit(solution)/shard_map/reduce_scatter | solution.py:255
  (24 other events, 465.8 us)
Sparse Core Ops, SparseCore 0:
  90.3 66.1 reduce-scatter.9
  159.5 43.8 all-gather.4
  205.9 43.6 all-gather.6
  257.9 65.9 reduce-scatter.13
  327.5 66.1 reduce-scatter.11
  396.6 45.2 all-gather.8
  496.2 62.1 reduce-scatter.15
  562.6 64.6 reduce-scatter.17
  629.7 79.8 reduce-scatter.21
  711.9 81.3 reduce-scatter.23
  795.7 81.3 reduce-scatter.25
  879.3 53.1 reduce-scatter.19
where the time goes:
time: 943 us; the launch traced here: 941 us
  waiting for transfers between devices  636 us (67%)
  blocking collectives  202 us (21%)
  matrix products  46.8 us (5%)
  other arithmetic  20.6 us (2%)
  local copies, waits for them, and re-layouts  18.9 us (2%)
  between operations  14.6 us (2%)
    reduce_scatter x1, waiting for transfers between devices, body(): lax.psum_scatter(col_terms[1].astype(jnp.bfloat16), 'ctx', scatter_dimens...  81.8 us
    reduce_scatter x1, waiting for transfers between devices, body(): lax.psum_scatter(row_terms[1].astype(jnp.bfloat16), 'ctx', scatter_dimens...  81.6 us
    reduce_scatter x1, waiting for transfers between devices, body(): lax.psum_scatter(row_terms[0].astype(jnp.bfloat16), 'ctx', scatter_dimens...  81 us
    reduce_scatter x1, waiting for transfers between devices, body(): lax.psum_scatter(jnp.dot(activated, w_down, preferred_element_type=jnp.fl...  67.8 us
    reduce_scatter x1, waiting for transfers between devices, body(): lax.psum_scatter(jnp.dot(attended_rows, w_out, preferred_element_type=jnp...  66.2 us
    psum x1, blocking collectives, body(): lax.psum(jnp.sum(grad_normed * hidden_f * inv_rms, axis=0), ('ctx', 'ffn'))  62.7 us
    reduce_scatter x1, waiting for transfers between devices, body(): lax.psum_scatter((jnp.dot(grad_gate, w_gate.T, preferred_element_type=jnp...  62.2 us
    reduce_scatter x1, waiting for transfers between devices, body(): lax.psum_scatter(col_terms[0].astype(jnp.bfloat16), 'ctx', scatter_dimens...  53.4 us
  transfers between devices with their start and end apart: 19, of which 17 were waited for; matrix products, arithmetic and copies ran while one was open for 5% of the time, Pallas kernels for 0%

commit v1 on v0

--- a/solution.py
+++ b/solution.py
@@ -152,7 +152,9 @@
         + inv_rms * gained
         - hidden_f * inv_cube * jnp.mean(gained * hidden_f, axis=1, keepdims=True)
     ).astype(jnp.bfloat16)
-    grad_gain = lax.psum(jnp.sum(grad_normed * hidden_f * inv_rms, axis=0), ("ctx", "ffn"))
+    grad_gain = jnp.sum(
+        lax.all_gather(jnp.sum(grad_normed * hidden_f * inv_rms, axis=0), ("ctx", "ffn")), axis=0
+    )
     grad_rows = lax.all_gather(grad_resid, "ffn", axis=0, tiled=True)
     grad_attended = jnp.dot(grad_rows, w_out.T, preferred_element_type=jnp.float32).astype(
         jnp.bfloat16

time: 943 us -> 1120 us (1.19)
  waiting for transfers between devices: 636 us -> 874 us
  blocking collectives: 202 us -> 140 us
    all_gather x0 -> x1, waiting for transfers between devices: none -> 196 us  [body(): lax.all_gather(jnp.sum(grad_normed * hidden_f * inv_rms, axis=0), ('ctx',...]
    psum x1 -> x0, blocking collectives: 62.7 us -> none  [body(): lax.psum(jnp.sum(grad_normed * hidden_f * inv_rms, axis=0), ('ctx', 'ffn'))]
    reduce_scatter x1, waiting for transfers between devices: 0.01 us -> 60.2 us  [body(): lax.psum_scatter(placed_key.astype(jnp.bfloat16), 'ffn', scatter_dimensio...]
    reduce_scatter x1, waiting for transfers between devices: 14.5 us -> 0.01 us  [body(): lax.psum_scatter(placed_value.astype(jnp.bfloat16), 'ffn', scatter_dimens...]
  transfers between devices with their start and end apart: 19 -> 20, of which waited for: 17 -> 18; matrix products, arithmetic and copies ran while one was open for 5% -> 4% of each run, Pallas kernels for 0% -> 0%
where the time goes in v1:
time: 1120 us
  waiting for transfers between devices  874 us (78%)
  blocking collectives  140 us (12%)
  matrix products  47.4 us (4%)
  other arithmetic  22.2 us (2%)
  local copies, waits for them, and re-layouts  20.2 us (2%)
  between operations  14.3 us (1%)
    all_gather x1, waiting for transfers between devices, body(): lax.all_gather(jnp.sum(grad_normed * hidden_f * inv_rms, axis=0), ('ctx',...  196 us
    reduce_scatter x1, waiting for transfers between devices, body(): lax.psum_scatter(row_terms[1].astype(jnp.bfloat16), 'ctx', scatter_dimens...  81.8 us
    reduce_scatter x1, waiting for transfers between devices, body(): lax.psum_scatter(col_terms[1].astype(jnp.bfloat16), 'ctx', scatter_dimens...  81.6 us
    reduce_scatter x1, waiting for transfers between devices, body(): lax.psum_scatter(row_terms[0].astype(jnp.bfloat16), 'ctx', scatter_dimens...  76.9 us
    reduce_scatter x1, waiting for transfers between devices, body(): lax.psum_scatter(jnp.dot(activated, w_down, preferred_element_type=jnp.fl...  67.8 us
    reduce_scatter x1, waiting for transfers between devices, body(): lax.psum_scatter(jnp.dot(attended_rows, w_out, preferred_element_type=jnp...  66.3 us
    reduce_scatter x1, waiting for transfers between devices, body(): lax.psum_scatter((jnp.dot(grad_gate, w_gate.T, preferred_element_type=jnp...  62.2 us
    reduce_scatter x1, waiting for transfers between devices, body(): lax.psum_scatter(placed_key.astype(jnp.bfloat16), 'ffn', scatter_dimensio...  60.2 us
  transfers between devices with their start and end apart: 20, of which 18 were waited for; matrix products, arithmetic and copies ran while one was open for 4% of the time, Pallas kernels for 0%

profile of v1, /device:TPU:32, one launch (start us, length us, event | category | flops | bytes accessed | tf_op | source)
XLA Modules:
  0.0 1119.9 jit_solution(6970376271682859031)
XLA Ops:
  9.5 19.0 %all-gather.1 = s32[8,1,128]{2,1,0:T(1,128)S(1)} all-gather(s32[1,1,128]{2,1,0:T(1,128)} %bitcast.186), channel_id=1, replica_groups=mesh['ctx'=8,'ffn'=16] {'ctx'}, dimensions={0}, use_global_device_ids=true | all-gather | bytes 4608 | tf_op jit(solution)/shard_map/all_gather | solution.py:64
  37.8 49.4 %while.21 = (s32[]{:T(128)}, f32[2,128]{1,0:T(2,128)S(1)}, f32[2,128]{1,0:T(2,128)S(1)}, f32[2,128,128]{2,1,0:T(8,128)S(1)}, bf16[128,2,128]{2,0,1:T(8,128)(2,1)...) while((s32[]{:T(128)}, f32[2,128]{1,0:T(2,128)S(1)}, ...), condition=%wide.region_5.6_spmd, body=%wide.region_2.5_spmd.sunk | while | flops 17187348 | bytes 1266056 | solution.py:101
  38.1 6.1 collective-permute-done
  45.1 6.6 collective-permute-done
  52.6 6.1 collective-permute-done
  59.6 6.1 collective-permute-done
  66.6 6.1 collective-permute-done
  73.5 6.1 collective-permute-done
  88.9 66.3 %reduce-scatter.10.cloned.1.call-done = bf16[8,4096]{1,0:T(8,128)(2,1)} async-done(((bf16[128,4096]{1,0:T(8,128)(2,1)}), bf16[8,4096]{1,0:T(8,128)(2,1)}) %reduce-scatter.10.cloned.1.call-update) | async-done | bytes 65552 | tf_op jit(solution)/shard_map/reduce_scatter | solution.py:109
  158.2 43.8 %all-gather.7.cloned.1.call-done = bf16[128,4096]{1,0:T(8,128)(2,1)} async-done(((bf16[8,4096]{1,0:T(8,128)(2,1)}), bf16[128,4096]{1,0:T(8,128)(2,1)}) %all-gather.7.cloned.1.call-update) | async-done | bytes 1048592 | tf_op jit(solution)/shard_map/all_gather | solution.py:119
  208.2 40.0 %all-gather.9.cloned.1.call-done = bf16[128,4096]{1,0:T(8,128)(2,1)} async-done(((bf16[8,4096]{1,0:T(8,128)(2,1)}), bf16[128,4096]{1,0:T(8,128)(2,1)}) %all-gather.9.cloned.1.call-update) | async-done | bytes 1048592 | tf_op jit(solution)/shard_map/all_gather | solution.py:133
  260.4 62.2 %reduce-scatter.14.cloned.1.call-done = bf16[8,4096]{1,0:T(8,128)(2,1)} async-done(((bf16[128,4096]{1,0:T(8,128)(2,1)}), bf16[8,4096]{1,0:T(8,128)(2,1)}) %reduce-scatter.14.cloned.1.call-update) | async-done | bytes 65552 | tf_op jit(solution)/shard_map/reduce_scatter | solution.py:139
  324.6 67.8 %reduce-scatter.12.cloned.1.call-done = bf16[8,4096]{1,0:T(8,128)(2,1)} async-done(((bf16[128,4096]{1,0:T(8,128)(2,1)}), bf16[8,4096]{1,0:T(8,128)(2,1)}) %reduce-scatter.12.cloned.1.call-update) | async-done | bytes 65552 | tf_op jit(solution)/shard_map/reduce_scatter | solution.py:126
  394.1 17.8 %all_gather.39 = f32[1024,2]{0,1:T(2,128)S(1)} all-gather(f32[128,2]{0,1:T(2,128)S(1)} %bitcast.190), channel_id=1, replica_groups=mesh['ctx'=8,'ffn'=16] {'ctx'}, dimensions={0}, use_global_device_ids=true | all-gather | bytes 9216 | tf_op jit(solution)/shard_map/all_gather | solution.py:170
  412.8 24.7 %all_gather.38 = bf16[1024,256]{0,1:T(8,128)(2,1)S(1)} all-gather(bf16[128,256]{0,1:T(8,128)(2,1)S(1)} %copy.61), channel_id=1, replica_groups=mesh['ctx'=8,'ffn'=16] {'ctx'}, dimensions={0}, use_global_device_ids=true | all-gather | bytes 589824 | tf_op jit(solution)/shard_map/all_gather | solution.py:197
  442.7 31.2 %all_gather.40 = bf16[1024,256]{1,0:T(8,128)(2,1)} all-gather(bf16[128,256]{1,0:T(8,128)(2,1)S(1)} %convolution_convert_fusion.6), channel_id=1, replica_groups=mesh['ctx'=8,'ffn'=16] {'ctx'}, dimensions={0}, use_global_device_ids=true | all-gather | bytes 589824 | tf_op jit(solution)/shard_map/all_gather | solution.py:198
  477.2 17.7 %all_gather.41 = f32[1024,2]{0,1:T(2,128)S(1)} all-gather(f32[128,2]{0,1:T(2,128)S(1)} %multiply_reduce_fusion), channel_id=1, replica_groups=mesh['ctx'=8,'ffn'=16] {'ctx'}, dimensions={0}, use_global_device_ids=true | all-gather | bytes 9216 | tf_op jit(solution)/shard_map/all_gather | solution.py:171
  514.3 29.2 %all_gather.36 = bf16[1024,2,128]{2,0,1:T(8,128)(2,1)S(1)} all-gather(bf16[128,2,128]{2,0,1:T(8,128)(2,1)S(1)} %copy-done.17), channel_id=1, replica_groups=mesh['ctx'=8,'ffn'=16] {'ctx'}, dimensions={0}, use_global_device_ids=true | all-gather | bytes 589824 | tf_op jit(solution)/shard_map/all_gather | solution.py:173
  549.4 60.2 %reduce-scatter.16.cloned.1.call-done = bf16[8,1024]{1,0:T(8,128)(2,1)} async-done(((bf16[128,1024]{1,0:T(8,128)(2,1)}), bf16[8,1024]{1,0:T(8,128)(2,1)}) %reduce-scatter.16.cloned.1.call-update) | async-done | bytes 16400 | tf_op jit(solution)/shard_map/reduce_scatter | solution.py:239
  610.9 195.6 %all-gather.13.cloned.1.call-done = f32[524288]{0:T(1024)} async-done(((f32[4096]{0:T(1024)}), f32[524288]{0:T(1024)}) %all-gather.13.cloned.1.call-update) | async-done | bytes 2097168 | tf_op jit(solution)/shard_map/all_gather | solution.py:156
  811.6 76.9 %reduce-scatter.22.cloned.1.call-done = bf16[512,448]{0,1:T(8,128)(2,1)} async-done(((bf16[4096,448]{0,1:T(8,128)(2,1)}), bf16[512,448]{0,1:T(8,128)(2,1)}) %reduce-scatter.22.cloned.1.call-update) | async-done | bytes 458768 | tf_op jit(solution)/shard_map/reduce_scatter | solution.py:248
  890.5 81.8 %reduce-scatter.24.cloned.1.call-done = bf16[512,448]{0,1:T(8,128)(2,1)} async-done(((bf16[4096,448]{0,1:T(8,128)(2,1)}), bf16[512,448]{0,1:T(8,128)(2,1)}) %reduce-scatter.24.cloned.1.call-update) | async-done | bytes 458768 | tf_op jit(solution)/shard_map/reduce_scatter | solution.py:251
  974.3 81.6 %reduce-scatter.26.cloned.1.call-done = bf16[448,512]{1,0:T(8,128)(2,1)} async-done(((bf16[448,4096]{1,0:T(8,128)(2,1)}), bf16[448,512]{1,0:T(8,128)(2,1)}) %reduce-scatter.26.cloned.1.call-update) | async-done | bytes 458768 | tf_op jit(solution)/shard_map/reduce_scatter | solution.py:260
  1058.0 53.5 %reduce-scatter.20.cloned.1.call-done = bf16[256,512]{1,0:T(8,128)(2,1)} async-done(((bf16[256,4096]{1,0:T(8,128)(2,1)}), bf16[256,512]{1,0:T(8,128)(2,1)}) %reduce-scatter.20.cloned.1.call-update) | async-done | bytes 262160 | tf_op jit(solution)/shard_map/reduce_scatter | solution.py:257
  (226 shorter events, 98.7 us)
Async XLA Ops:
  7.2 80.1 %copy-start = (bf16[256,4096]{1,0:T(8,128)(2,1)S(1)}, bf16[256,4096]{1,0:T(8,128)(2,1)}, u32[]{:S(2)}) copy-start(bf16[256,4096]{1,0:T(8,128)(2,1)} %param.18) | copy-start | bytes 6291460
  7.2 147.9 %reduce-scatter.10.cloned.1.call-start = ((), (), s32[]{:S(2)}) async-start(), calls=%async_computation.9 | async-start | bytes 1114112 | tf_op jit(solution)/shard_map/reduce_scatter | solution.py:109
  37.8 6.4 collective-permute-start
  44.8 6.9 collective-permute-start
  52.2 6.4 collective-permute-start
  59.2 6.4 collective-permute-start
  66.2 6.4 collective-permute-start
  73.2 6.4 collective-permute-start
  80.2 6.4 collective-permute-start
  87.1 71.1 %copy-start.23 = (s32[128]{0:T(128)}, s32[128]{0:T(128)S(1)}, u32[]{:S(2)}) copy-start(s32[128]{0:T(128)S(1)} %get-tuple-element.587) | copy-start | bytes 1540
  87.1 71.1 %copy-start.25 = (s32[1024]{0:T(1024)}, s32[1024]{0:T(1024)S(1)}, u32[]{:S(2)}) copy-start(s32[1024]{0:T(1024)S(1)} %get-tuple-element.588) | copy-start | bytes 12292
  88.8 113.2 %all-gather.7.cloned.1.call-start = ((), (), s32[]{:S(2)}) async-start(), calls=%async_computation.10 | async-start | bytes 1114112 | tf_op jit(solution)/shard_map/all_gather | solution.py:119
  157.4 90.8 %all-gather.9.cloned.1.call-start = ((), (), s32[]{:S(2)}) async-start(), calls=%async_computation.12 | async-start | bytes 1114112 | tf_op jit(solution)/shard_map/all_gather | solution.py:133
  158.1 164.4 %reduce-scatter.14.cloned.1.call-start = ((), (), s32[]{:S(2)}) async-start(), calls=%async_computation.13 | async-start | bytes 1114112 | tf_op jit(solution)/shard_map/reduce_scatter | solution.py:139
  256.4 136.0 %copy-start.18 = (bf16[8,4096]{1,0:T(8,128)(2,1)S(1)}, bf16[8,4096]{1,0:T(8,128)(2,1)}, u32[]{:S(2)}) copy-start(bf16[8,4096]{1,0:T(8,128)(2,1)} %param.23) | copy-start | bytes 196612
  256.4 135.9 %reduce-scatter.12.cloned.1.call-start = ((), (), s32[]{:S(2)}) async-start(), calls=%async_computation.11 | async-start | bytes 1114112 | tf_op jit(solution)/shard_map/reduce_scatter | solution.py:126
  260.3 180.3 %all-gather.11.cloned.1.call-start = ((), (), s32[]{:S(2)}) async-start(), calls=%async_computation.14 | async-start | bytes 1114112 | tf_op jit(solution)/shard_map/all_gather | solution.py:158
  394.0 154.0 %reduce-scatter.18.cloned.1.call-start = ((), (), s32[]{:S(2)}) async-start(), calls=%async_computation.16 | async-start | bytes 278528 | tf_op jit(solution)/shard_map/reduce_scatter | solution.py:242
  477.1 132.5 %reduce-scatter.16.cloned.1.call-start = ((), (), s32[]{:S(2)}) async-start(), calls=%async_computation.15 | async-start | bytes 278528 | tf_op jit(solution)/shard_map/reduce_scatter | solution.py:239
  497.8 308.8 %all-gather.13.cloned.1.call-start = ((), (), s32[]{:S(2)}) async-start(), calls=%async_computation.21 | async-start | bytes 2113536 | tf_op jit(solution)/shard_map/all_gather | solution.py:156
  498.5 389.9 %reduce-scatter.22.cloned.1.call-start = ((), (), s32[]{:S(2)}) async-start(), calls=%async_computation.18 | async-start | bytes 4128768 | tf_op jit(solution)/shard_map/reduce_scatter | solution.py:248
  502.6 469.7 %reduce-scatter.24.cloned.1.call-start = ((), (), s32[]{:S(2)}) async-start(), calls=%async_computation.19 | async-start | bytes 4128768 | tf_op jit(solution)/shard_map/reduce_scatter | solution.py:251
  506.4 549.5 %reduce-scatter.26.cloned.1.call-start = ((), (), s32[]{:S(2)}) async-start(), calls=%async_computation.20 | async-start | bytes 4128768 | tf_op jit(solution)/shard_map/reduce_scatter | solution.py:260
  510.7 600.8 %reduce-scatter.20.cloned.1.call-start = ((), (), s32[]{:S(2)}) async-start(), calls=%async_computation.17 | async-start | bytes 2359296 | tf_op jit(solution)/shard_map/reduce_scatter | solution.py:257
  (26 other events, 428.4 us)
Sparse Core Ops, SparseCore 0:
  88.9 66.1 reduce-scatter.9
  158.2 43.8 all-gather.6
  204.5 43.6 all-gather.8
  256.5 65.9 reduce-scatter.13
  326.1 66.1 reduce-scatter.11
  395.2 45.2 all-gather.10
  477.2 63.4 reduce-scatter.17
  544.9 64.6 reduce-scatter.15
  611.9 194.6 all-gather.12
  808.8 79.6 reduce-scatter.21
  890.9 81.3 reduce-scatter.23
  974.6 81.3 reduce-scatter.25
  1058.3 53.1 reduce-scatter.19
